TPU v7x, 32 devices: a whole 2x2x4 slice. The times are simulated.
32 devices in a mesh: season: 2 (over core), cells: 16 (over z, y, x).
Axes of the slice: x: 2, y: 2, z: 4, core: 2. Of those that a mesh axis runs over, the one named last changes fastest.
Arguments:
- start_adjoint: float32 [2, 8, 32768], P('season', None, 'cells'), may hold values from -6 to 6
- adjoint_tiles: bfloat16 [2, 2, 256, 3, 128, 128], P('season', None, 'cells'), may hold values from -0.21875 to 0.21875
- column_tiles: int32 [2, 2, 256, 3], P('season', None, 'cells'), may hold values from 0 to 255, as said below
- source_jacobian: float32 [2, 2, 8, 8, 32768], P('season', None, None, None, 'cells'), may hold values from -0.9 to 0.9
- obs_owner: int32 [2, 4096, 1], P('season', 'cells'), may hold values from 0 to 15; in each aligned block of 256 rows (0 to 255, 256 to 511, ..., all dimensions but the last counted through in order) at most 32 rows name the same one
- obs_local: int32 [2, 4096], P('season', 'cells'), may hold values from 0 to 2047
- obs_day: int32 [2, 4096], P('season', 'cells'), may hold values from 0 to 1
- obs_tracer: int32 [2, 4096], P('season', 'cells'), may hold values from 0 to 7
- obs_misfit: float32 [2, 4096], P('season', 'cells'), may hold values from -6 to 6
Outputs:
- start_update: float32 [2, 8, 32768], P('season', None, 'cells')
Inputs may be any that keep to these rules, and one draw needn't show every extreme that they name: `column_tiles`: entry [s, m, t, 0] equals t; every other entry lies within 8 tiles of t on the closed range of 256 tiles, indices taken modulo 256. `obs_owner`: in each aligned block of 256 observations (the list of one device) no owner is named more than 32 times, a bound that some block reaches.
All inputs are finite; a program needn't handle non-finite values.
Results may differ from a plain program's by a relative error of at most 0.0003.
Values sent between devices are 32-bit elements; how exact they have to be, the bound alone decides.
A program may use at most 64 MiB of HBM per device.

v0:
```python
import jax
import jax.numpy as jnp
from jax import lax
from jax.sharding import PartitionSpec as P

NB = 3
DAYS = 2
REACH = 8


def with_halo(cells, sides, width):
    for axis, dim in sides:
        count = lax.axis_size(axis)
        head = lax.slice_in_dim(cells, 0, width, axis=dim)
        tail = lax.slice_in_dim(cells, cells.shape[dim] - width, cells.shape[dim], axis=dim)
        cells = jnp.concatenate(
            [
                lax.ppermute(tail, axis, [(i, (i + 1) % count) for i in range(count)]),
                cells,
                lax.ppermute(head, axis, [((i + 1) % count, i) for i in range(count)]),
            ],
            axis=dim,
        )
    return cells


def from_behind(value, axis, steps):
    count = lax.axis_size(axis)
    pairs = [(source, (source + steps) % count) for source in range(count)]
    return lax.ppermute(value, axis, pairs)


def on_device(
    start_adjoint,
    adjoint_tiles,
    column_tiles,
    source_jacobian,
    obs_owner,
    obs_local,
    obs_day,
    obs_tracer,
    obs_misfit,
):
    peer_count = lax.axis_size("cells")
    own_index = lax.axis_index("cells")
    tracers = start_adjoint.shape[1]
    cells_here = start_adjoint.shape[2]
    tiles_here = adjoint_tiles.shape[2]
    tile_rows = adjoint_tiles.shape[-1]
    total_tiles = tiles_here * peer_count
    forcing_slots = DAYS * tracers * cells_here

    def apply_matrix(matrix_tiles, column_ids, adjoint_field):
        widened = with_halo(adjoint_field, (("cells", 1),), REACH * tile_rows)
        blocks = widened.reshape(tracers, tiles_here + 2 * REACH, tile_rows)
        local_ids = (column_ids - own_index * tiles_here + REACH) % total_tiles
        picked = jnp.take(blocks, local_ids.reshape(-1), axis=1).reshape(
            tracers, tiles_here, NB, tile_rows
        )
        product = jnp.einsum(
            "tkac,rtkc->rta",
            matrix_tiles,
            picked,
            preferred_element_type=jnp.float32,
            precision=lax.Precision.HIGHEST,
        )
        return adjoint_field + product.reshape(tracers, cells_here)

    station_owner = obs_owner[0, :, 0]
    slot_key = ((obs_day[0] * tracers + obs_tracer[0]) * cells_here + obs_local[0]).astype(
        jnp.float32
    )
    packed = jnp.stack([station_owner.astype(jnp.float32), slot_key, obs_misfit[0]], axis=0)
    everything = lax.all_gather(packed, "cells", axis=1, tiled=True)
    mine = everything[0].astype(jnp.int32) == own_index
    arrived_keys = jnp.where(mine, everything[1].astype(jnp.int32), 0)
    arrived_values = jnp.where(mine, everything[2], 0.0)
    forcing = jax.ops.segment_sum(arrived_values, arrived_keys, num_segments=forcing_slots).reshape(
        DAYS, tracers, cells_here
    )
    adjoint = from_behind(start_adjoint[0], "season", -1)
    for day_index in reversed(range(DAYS)):
        carried = apply_matrix(adjoint_tiles[0, 0], column_tiles[0, 0], adjoint)
        coupled = jnp.einsum(
            "jrc,jc->rc", source_jacobian[0, day_index], carried, precision=lax.Precision.HIGHEST
        )
        adjoint = (
            apply_matrix(adjoint_tiles[0, 1], column_tiles[0, 1], carried)
            + coupled
            + forcing[day_index]
        )
    return adjoint[None]


def solution(mesh):
    placed = (
        P("season", None, "cells"),
        P("season", None, "cells", None, None, None),
        P("season", None, "cells", None),
        P("season", None, None, None, "cells"),
        P("season", "cells", None),
        P("season", "cells"),
        P("season", "cells"),
        P("season", "cells"),
        P("season", "cells"),
    )
    return jax.shard_map(
        on_device, mesh=mesh, in_specs=placed, out_specs=P("season", None, "cells"), check_vma=False
    )
```

profile of v0, /device:TPU:0, one launch (start us, length us, event | category | flops | bytes accessed | tf_op | source)
XLA Modules:
  0.0 120.8 jit_solution(8678704159165048102)
XLA Ops:
  0.0 0.5 collective-permute-start
  0.5 0.9 convert_bitcast_fusion
  1.4 0.7 add_convert_fusion
  2.1 0.7 pad_maximum_fusion
  2.8 42.3 %all_gather.3 = f32[3,4096]{1,0:T(4,128)S(1)} all-gather(f32[3,256]{1,0:T(4,128)S(1)} %pad_maximum_fusion), channel_id=1, replica_groups=mesh['season'=2,'cells'=16] {'cells'}, dimensions={1}, use_global_device_ids=true | all-gather | bytes 52224 | tf_op jit(solution)/shard_map/all_gather | solution.py:74
  45.2 27.9 %scatter_custom_fusion = f32[32768]{0:T(1024)S(1)} fusion(s32[4096]{0:T(1024)S(1)} %bitcast.115, f32[4096]{0:T(1024)S(1)} %bitcast.116, f32[]{:T(128)} %constant.49.clone.1), kind=kCustom, calls=%fused_computation.38 | custom fusion | flops 4096 | bytes 131076 | tf_op jit(solution)/shard_map/scatter-add | solution.py:78
  73.1 0.6 fusion.25
  73.8 0.8 fusion.30
  75.0 2.0 %collective-permute-start.1 = (f32[8,1024]{1,0:T(8,128)S(1)}, f32[8,1024]{1,0:T(8,128)S(1)}, u32[]{:S(2)}, u32[]{:S(2)}) collective-permute-start(f32[8,1024]{1,0:T(8,128)S(1)} %get-tuple-element.18), channel_id=1, source_target_pairs={{0,1},{1,2},{2,3},{3,4},{4,5},{5,6},{6,7},{7,8},{8,9},{9,10},{10,1... | collective-permute-start | bytes 98312 | tf_op jit(solution)/shard_map/ppermute | solution.py:18
  77.0 0.6 slice.96
  77.7 1.2 %collective-permute-done.2 = f32[8,1024]{1,0:T(8,128)S(1)} collective-permute-done((f32[8,1024]{1,0:T(8,128)S(1)}, f32[8,1024]{1,0:T(8,128)S(1)}, u32[]{:S(2)}, u32[]{:S(2)}) %collective-permute-start.2) | collective-permute-done | bytes 32800 | tf_op jit(solution)/shard_map/ppermute | solution.py:20
  78.9 3.7 %collective-permute-done.1 = f32[8,1024]{1,0:T(8,128)S(1)} collective-permute-done((f32[8,1024]{1,0:T(8,128)S(1)}, f32[8,1024]{1,0:T(8,128)S(1)}, u32[]{:S(2)}, u32[]{:S(2)}) %collective-permute-start.1) | collective-permute-done | bytes 32800 | tf_op jit(solution)/shard_map/ppermute | solution.py:18
  82.6 0.6 gather_fusion
  83.3 3.1 %fusion.8 = f32[8,2048]{1,0:T(8,128)S(1)} fusion(f32[8,2048]{1,0:T(8,128)S(1)} %collective-permute-done, f32[8,16,3,128]{3,0,2,1:T(8,128)S(1)} %bitcast.112, bf16[1,2,16,3,128,128]{5,4,3,2,1,0:T(8,128)(2,1)} %param.12), kind=kOutput, calls=%fused_computation.17 | convolution fusion | flops 75513856 | bytes 1900544 | tf_op jit(solution)/shard_map/tkac,rtkc->rta/dot_general | solution.py:60
  86.6 2.0 %collective-permute-start.3 = (f32[8,1024]{1,0:T(8,128)S(1)}, f32[8,1024]{1,0:T(8,128)S(1)}, u32[]{:S(2)}, u32[]{:S(2)}) collective-permute-start(f32[8,1024]{1,0:T(8,128)S(1)} %get-tuple-element.16), channel_id=1, source_target_pairs={{0,1},{1,2},{2,3},{3,4},{4,5},{5,6},{6,7},{7,8},{8,9},{9,10},{10,1... | collective-permute-start | bytes 98312 | tf_op jit(solution)/shard_map/ppermute | solution.py:18
  88.6 1.7 %fusion.18 = f32[2048,8]{0,1:T(8,128)} fusion(f32[1,2,8,8,2048]{4,3,2,1,0:T(8,128)} %param.14, f32[2048,8]{0,1:T(8,128)S(1)} %bitcast.110), kind=kLoop, calls=%fused_computation.29 | loop fusion | flops 245760 | bytes 655360 | tf_op jit(solution)/shard_map/jrc,jc->rc/dot_general | solution.py:84
  90.3 0.2 collective-permute-done.4
  90.5 3.7 %collective-permute-done.3 = f32[8,1024]{1,0:T(8,128)S(1)} collective-permute-done((f32[8,1024]{1,0:T(8,128)S(1)}, f32[8,1024]{1,0:T(8,128)S(1)}, u32[]{:S(2)}, u32[]{:S(2)}) %collective-permute-start.3) | collective-permute-done | bytes 32800 | tf_op jit(solution)/shard_map/ppermute | solution.py:18
  94.1 0.6 gather_fusion.1
  94.9 2.6 %fusion.7 = f32[8,2048]{1,0:T(8,128)S(1)} fusion(f32[8,2048]{1,0:T(8,128)} %slice.96, f32[8,2048]{1,0:T(8,128)S(1)} %fusion.8, f32[8,16,3,128]{3,0,2,1:T(8,128)S(1)} %bitcast.114, bf16[1,2,16,3,128,128]{5,4,3,2,1,0:T(8,128)(2,1)S(1)} %copy-done, f32[2048,8]{0,1:T(8,128)} %fusion.18), kind=kOutput, calls=%fused_computation.15 | convolution fusion | flops 75546624 | bytes 2031616 | tf_op jit(solution)/shard_map/tkac,rtkc->rta/dot_general | solution.py:60
  97.6 2.0 %collective-permute-start.5 = (f32[8,1024]{1,0:T(8,128)S(1)}, f32[8,1024]{1,0:T(8,128)S(1)}, u32[]{:S(2)}, u32[]{:S(2)}) collective-permute-start(f32[8,1024]{1,0:T(8,128)S(1)} %get-tuple-element.14), channel_id=1, source_target_pairs={{0,1},{1,2},{2,3},{3,4},{4,5},{5,6},{6,7},{7,8},{8,9},{9,10},{10,1... | collective-permute-start | bytes 98312 | tf_op jit(solution)/shard_map/ppermute | solution.py:18
  99.6 1.5 %slice.103 = f32[8,2048]{1,0:T(8,128)} reshape(f32[16384]{0:T(1024)} %get-tuple-element.11) | data formatting | bytes 131072 | tf_op jit(solution)/shard_map/slice | solution.py:90
  101.1 0.4 collective-permute-done.6
  101.5 3.7 %collective-permute-done.5 = f32[8,1024]{1,0:T(8,128)S(1)} collective-permute-done((f32[8,1024]{1,0:T(8,128)S(1)}, f32[8,1024]{1,0:T(8,128)S(1)}, u32[]{:S(2)}, u32[]{:S(2)}) %collective-permute-start.5) | collective-permute-done | bytes 32800 | tf_op jit(solution)/shard_map/ppermute | solution.py:18
  105.1 1.3 %gather_fusion.2 = f32[48,8,128]{2,1,0:T(8,128)} fusion(f32[8,32,128]{2,0,1:T(8,128)S(1)} %maximum_bitcast_fusion.2, s32[1024]{0:T(1024)S(1)} %pad_clamp_fusion.1), kind=kCustom, calls=%fused_computation.2.clone | custom fusion | bytes 393408 | tf_op jit(solution)/shard_map/jit(_take)/gather | solution.py:57
  106.4 1.0 broadcast_select_fusion.1
  107.5 1.7 %fusion.4 = f32[8,2048]{1,0:T(8,128)S(1)} fusion(f32[8,2048]{1,0:T(8,128)S(1)} %fusion.7, f32[8,16,3,128]{3,0,2,1:T(8,128)S(1)} %bitcast.111, bf16[1,2,16,3,128,128]{5,4,3,2,1,0:T(8,128)(2,1)S(1)} %copy-done), kind=kOutput, calls=%fused_computation.11 | convolution fusion | flops 75513856 | bytes 1900544 | tf_op jit(solution)/shard_map/tkac,rtkc->rta/dot_general | solution.py:60
  109.3 2.0 %collective-permute-start.7 = (f32[8,1024]{1,0:T(8,128)S(1)}, f32[8,1024]{1,0:T(8,128)S(1)}, u32[]{:S(2)}, u32[]{:S(2)}) collective-permute-start(f32[8,1024]{1,0:T(8,128)S(1)} %get-tuple-element.12), channel_id=1, source_target_pairs={{0,1},{1,2},{2,3},{3,4},{4,5},{5,6},{6,7},{7,8},{8,9},{9,10},{10,1... | collective-permute-start | bytes 98312 | tf_op jit(solution)/shard_map/ppermute | solution.py:18
  111.3 1.7 %fusion.17 = f32[2048,8]{0,1:T(8,128)} fusion(f32[1,2,8,8,2048]{4,3,2,1,0:T(8,128)} %param.14, f32[2048,8]{0,1:T(8,128)S(1)} %bitcast.109), kind=kLoop, calls=%fused_computation.27 | loop fusion | flops 245760 | bytes 655360 | tf_op jit(solution)/shard_map/jrc,jc->rc/dot_general | solution.py:84
  113.2 3.7 %collective-permute-done.7 = f32[8,1024]{1,0:T(8,128)S(1)} collective-permute-done((f32[8,1024]{1,0:T(8,128)S(1)}, f32[8,1024]{1,0:T(8,128)S(1)}, u32[]{:S(2)}, u32[]{:S(2)}) %collective-permute-start.7) | collective-permute-done | bytes 32800 | tf_op jit(solution)/shard_map/ppermute | solution.py:18
  116.8 0.6 gather_fusion.3
  117.6 3.2 %fusion.3 = f32[1,8,2048]{2,1,0:T(8,128)} fusion(f32[8,2048]{1,0:T(8,128)} %slice.103, f32[8,2048]{1,0:T(8,128)S(1)} %fusion.4, f32[8,16,3,128]{3,0,2,1:T(8,128)S(1)} %bitcast.113, bf16[1,2,16,3,128,128]{5,4,3,2,1,0:T(8,128)(2,1)S(1)} %copy-done, f32[2048,8]{0,1:T(8,128)} %fusion.17), kind=kOutput, calls=%fused_computation.9 | convolution fusion | flops 75546624 | bytes 2031616 | tf_op jit(solution)/shard_map/tkac,rtkc->rta/dot_general | solution.py:60
  (30 shorter events, 1.3 us)
Async XLA Ops:
  0.0 94.9 %copy-start = (bf16[1,2,16,3,128,128]{5,4,3,2,1,0:T(8,128)(2,1)S(1)}, bf16[1,2,16,3,128,128]{5,4,3,2,1,0:T(8,128)(2,1)}, u32[]{:S(2)}) copy-start(bf16[1,2,16,3,128,128]{5,4,3,2,1,0:T(8,128)(2,1)} %param.12) | copy-start | bytes 9437188
  0.0 74.9 %collective-permute-start = (f32[8,2048]{1,0:T(8,128)}, f32[8,2048]{1,0:T(8,128)S(1)}, u32[]{:S(2)}, u32[]{:S(2)}) collective-permute-start(f32[8,2048]{1,0:T(8,128)} %bitcast.117), channel_id=1, source_target_pairs={{0,16},{16,0},{1,17},{17,1},{2,18},{18,2},{3,19},{19,3},{4,20},{20... | collective-permute-start | bytes 196616 | tf_op jit(solution)/shard_map/ppermute | solution.py:30
  75.0 4.0 %collective-permute-start.2 = (f32[8,1024]{1,0:T(8,128)S(1)}, f32[8,1024]{1,0:T(8,128)S(1)}, u32[]{:S(2)}, u32[]{:S(2)}) collective-permute-start(f32[8,1024]{1,0:T(8,128)S(1)} %get-tuple-element.19), channel_id=1, source_target_pairs={{1,0},{2,1},{3,2},{4,3},{5,4},{6,5},{7,6},{8,7},{9,8},{10,9},{11,1... | collective-permute-start | bytes 98312 | tf_op jit(solution)/shard_map/ppermute | solution.py:20
  75.0 7.6 %collective-permute-start.1 = (f32[8,1024]{1,0:T(8,128)S(1)}, f32[8,1024]{1,0:T(8,128)S(1)}, u32[]{:S(2)}, u32[]{:S(2)}) collective-permute-start(f32[8,1024]{1,0:T(8,128)S(1)} %get-tuple-element.18), channel_id=1, source_target_pairs={{0,1},{1,2},{2,3},{3,4},{4,5},{5,6},{6,7},{7,8},{8,9},{9,10},{10,1... | collective-permute-start | bytes 98312 | tf_op jit(solution)/shard_map/ppermute | solution.py:18
  86.5 4.0 %collective-permute-start.4 = (f32[8,1024]{1,0:T(8,128)S(1)}, f32[8,1024]{1,0:T(8,128)S(1)}, u32[]{:S(2)}, u32[]{:S(2)}) collective-permute-start(f32[8,1024]{1,0:T(8,128)S(1)} %get-tuple-element.17), channel_id=1, source_target_pairs={{1,0},{2,1},{3,2},{4,3},{5,4},{6,5},{7,6},{8,7},{9,8},{10,9},{11,1... | collective-permute-start | bytes 98312 | tf_op jit(solution)/shard_map/ppermute | solution.py:20
  86.6 7.6 %collective-permute-start.3 = (f32[8,1024]{1,0:T(8,128)S(1)}, f32[8,1024]{1,0:T(8,128)S(1)}, u32[]{:S(2)}, u32[]{:S(2)}) collective-permute-start(f32[8,1024]{1,0:T(8,128)S(1)} %get-tuple-element.16), channel_id=1, source_target_pairs={{0,1},{1,2},{2,3},{3,4},{4,5},{5,6},{6,7},{7,8},{8,9},{9,10},{10,1... | collective-permute-start | bytes 98312 | tf_op jit(solution)/shard_map/ppermute | solution.py:18
  97.5 4.0 %collective-permute-start.6 = (f32[8,1024]{1,0:T(8,128)S(1)}, f32[8,1024]{1,0:T(8,128)S(1)}, u32[]{:S(2)}, u32[]{:S(2)}) collective-permute-start(f32[8,1024]{1,0:T(8,128)S(1)} %get-tuple-element.15), channel_id=1, source_target_pairs={{1,0},{2,1},{3,2},{4,3},{5,4},{6,5},{7,6},{8,7},{9,8},{10,9},{11,1... | collective-permute-start | bytes 98312 | tf_op jit(solution)/shard_map/ppermute | solution.py:20
  97.6 7.6 %collective-permute-start.5 = (f32[8,1024]{1,0:T(8,128)S(1)}, f32[8,1024]{1,0:T(8,128)S(1)}, u32[]{:S(2)}, u32[]{:S(2)}) collective-permute-start(f32[8,1024]{1,0:T(8,128)S(1)} %get-tuple-element.14), channel_id=1, source_target_pairs={{0,1},{1,2},{2,3},{3,4},{4,5},{5,6},{6,7},{7,8},{8,9},{9,10},{10,1... | collective-permute-start | bytes 98312 | tf_op jit(solution)/shard_map/ppermute | solution.py:18
  109.2 4.0 %collective-permute-start.8 = (f32[8,1024]{1,0:T(8,128)S(1)}, f32[8,1024]{1,0:T(8,128)S(1)}, u32[]{:S(2)}, u32[]{:S(2)}) collective-permute-start(f32[8,1024]{1,0:T(8,128)S(1)} %get-tuple-element.13), channel_id=1, source_target_pairs={{1,0},{2,1},{3,2},{4,3},{5,4},{6,5},{7,6},{8,7},{9,8},{10,9},{11,1... | collective-permute-start | bytes 98312 | tf_op jit(solution)/shard_map/ppermute | solution.py:20
  109.3 7.6 %collective-permute-start.7 = (f32[8,1024]{1,0:T(8,128)S(1)}, f32[8,1024]{1,0:T(8,128)S(1)}, u32[]{:S(2)}, u32[]{:S(2)}) collective-permute-start(f32[8,1024]{1,0:T(8,128)S(1)} %get-tuple-element.12), channel_id=1, source_target_pairs={{0,1},{1,2},{2,3},{3,4},{4,5},{5,6},{6,7},{7,8},{8,9},{9,10},{10,1... | collective-permute-start | bytes 98312 | tf_op jit(solution)/shard_map/ppermute | solution.py:18
where the time goes:
time: 121 us
  blocking collectives  42.3 us (35%)
  other arithmetic  35.2 us (29%)
  waiting for transfers between devices  16.6 us (14%)
  matrix products  10.7 us (9%)
  starting transfers between devices  8.78 us (7%)
  local copies, waits for them, and re-layouts  7.01 us (6%)
    all_gather x1, blocking collectives, on_device(): everything = lax.all_gather(packed, 'cells', axis=1, tiled=True)  42.3 us
    scatter-add x1, other arithmetic, on_device(): jax.ops.segment_sum(arrived_values, arrived_keys, num_segments=forcing_sl...  27.9 us
    ppermute x4, waiting for transfers between devices, with_halo(): lax.ppermute(tail, axis, [(i, (i + 1) % count) for i in range(count)])  14.6 us
    dot_general x4, matrix products, apply_matrix(): jnp.einsum('tkac,rtkc->rta', matrix_tiles, picked, preferred_element_type...  10.7 us
    ppermute x4, starting transfers between devices, with_halo(): lax.ppermute(tail, axis, [(i, (i + 1) % count) for i in range(count)])  8.05 us
    dot_general x2, other arithmetic, on_device(): jnp.einsum('jrc,jc->rc', source_jacobian[0, day_index], carried, precisio...  3.44 us
    gather x4, local copies, waits for them, and re-layouts, apply_matrix(): jnp.take(blocks, local_ids.reshape(-1), axis=1)  3.11 us
    slice x3, local copies, waits for them, and re-layouts, on_device(): forcing[day_index]  2.76 us
  transfers between devices with their start and end apart: 9, of which 8 were waited for; matrix products, arithmetic and copies ran while one was open for 31% of the time, Pallas kernels for 0%

commit v1 on v0

v1 whole, which is shorter than its diff:
```python
import functools

import jax
import jax.numpy as jnp
from jax import lax
from jax.experimental import pallas as pl
from jax.experimental.pallas import tpu as pltpu
from jax.sharding import PartitionSpec as P

REACH = 8
MESH = pl.DeviceIdType.MESH
F32 = jnp.float32
BF16 = jnp.bfloat16


def dot_nt(a, b):
    return lax.dot_general(a, b, (((1,), (1,)), ((), ())), preferred_element_type=F32)


def kernel(
    seasons,
    peers,
    cols_ref,
    start_ref,
    tiles_hbm,
    jac_hbm,
    owner_ref,
    local_ref,
    day_ref,
    tracer_ref,
    misfit_ref,
    out_ref,
    tiles_vm,
    jac_vm,
    wide,
    packed,
    base,
    obs,
    force,
    load_sem,
    send_sem,
    recv_sem,
    obs_send_sem,
    obs_recv_sem,
):
    s = lax.axis_index("season")
    c = lax.axis_index("cells")
    days, tracers = jac_vm.shape[0], jac_vm.shape[1]
    tiles_here, near = tiles_vm.shape[1], tiles_vm.shape[2]
    rows = tiles_vm.shape[-1]
    cells_here = tiles_here * rows
    halo = REACH * rows
    rounds = 2 * days
    own = slice(halo, halo + cells_here)

    loads = [
        pltpu.make_async_copy(tiles_hbm.at[0, 0], tiles_vm.at[0], load_sem.at[0]),
        pltpu.make_async_copy(tiles_hbm.at[0, 1], tiles_vm.at[1], load_sem.at[1]),
        pltpu.make_async_copy(jac_hbm.at[0], jac_vm, load_sem.at[2]),
    ]
    for load in loads:
        load.start()

    met = {(0, o) for o in range(1, peers)}
    met |= {(ds % seasons, dc % peers) for ds in (1, -1) for dc in (-1, 0, 1)}
    met = sorted(met - {(0, 0)})
    barrier = pltpu.get_barrier_semaphore()
    for ds, dc in met:
        pl.semaphore_signal(
            barrier,
            inc=1,
            device_id=(lax.rem(s + ds, seasons), lax.rem(c + dc, peers)),
            device_id_type=MESH,
        )

    shift = rows.bit_length() - 1
    local = local_ref[...]
    row_key = (local >> shift) * (days * tracers) + day_ref[...] * tracers + tracer_ref[...]
    fields = (
        owner_ref[...].astype(F32),
        row_key.astype(F32),
        (local & (rows - 1)).astype(F32),
        misfit_ref[...],
    )
    lists = local.shape[1] // rows
    pieces = [f[:, i * rows : (i + 1) * rows] for f in fields for i in range(lists)]
    obs[0] = jnp.concatenate(pieces, axis=0)

    left, right = lax.rem(c + peers - 1, peers), lax.rem(c + 1, peers)
    before = lax.rem(s + seasons - 1, seasons)

    def copy(src, r, lanes, season, cell, which):
        return pltpu.make_async_remote_copy(
            src_ref=src,
            dst_ref=wide.at[r, :, lanes],
            send_sem=send_sem.at[r, which],
            recv_sem=recv_sem.at[r, which],
            device_id=(season, cell),
            device_id_type=MESH,
        )

    def halo_copies(r):
        season = before if r == 0 else s
        if r == 0:
            head = start_ref.at[0, :, 0:halo]
            tail = start_ref.at[0, :, cells_here - halo : cells_here]
        else:
            head = wide.at[r, :, halo : 2 * halo]
            tail = wide.at[r, :, cells_here : halo + cells_here]
        return (
            copy(head, r, slice(halo + cells_here, 2 * halo + cells_here), season, left, 0),
            copy(tail, r, slice(0, halo), season, right, 1),
        )

    def obs_copy(o):
        return pltpu.make_async_remote_copy(
            src_ref=obs.at[0],
            dst_ref=obs.at[o],
            send_sem=obs_send_sem.at[o],
            recv_sem=obs_recv_sem.at[o],
            device_id=(s, lax.rem(c + o, peers)),
            device_id_type=MESH,
        )

    sends = [halo_copies(r) for r in range(rounds)]
    body = copy(start_ref.at[0], 0, own, before, c, 2)

    pl.semaphore_wait(barrier, len(met))
    sends[0][0].start()
    sends[0][1].start()
    body.start()

    @pl.loop(1, peers)
    def _(o):
        obs_copy(o).start()

    def pack(r, first, count):
        for t in range(first, first + count):
            v = wide[r, :, at_tile(t)]
            high = v.astype(BF16).astype(F32)
            packed[t] = jnp.concatenate([high, v - high], axis=0).astype(BF16)

    def gather_forcing():
        row_ids = lax.broadcasted_iota(jnp.int32, (force.shape[0], rows), 0).astype(F32)
        lane_ids = lax.broadcasted_iota(jnp.int32, (rows, rows), 0).astype(F32)
        here = c.astype(F32)
        force[...] = jnp.zeros_like(force)

        @pl.loop(0, peers)
        def _(o):
            @pl.when(o > 0)
            def _():
                obs_copy(o).wait_recv()

            block = obs[o]
            slots, values = [], []
            for i in range(lists):
                owner = block[i : i + 1]
                row = jnp.where(owner == here, block[lists + i : lists + i + 1], -1.0)
                lane = block[2 * lists + i : 2 * lists + i + 1]
                misfit = block[3 * lists + i : 3 * lists + i + 1]
                high = misfit.astype(BF16).astype(F32)
                hit = lane_ids == lane
                slots.append(jnp.where(row_ids == row, 1.0, 0.0).astype(BF16))
                values.append(
                    jnp.concatenate(
                        [jnp.where(hit, high, 0.0), jnp.where(hit, misfit - high, 0.0)], axis=0
                    ).astype(BF16)
                )
            force[...] += dot_nt(
                jnp.concatenate(slots, axis=1), jnp.concatenate(values, axis=1)
            )

    def at_tile(t):
        return slice(t * rows, (t + 1) * rows)

    def shifted(t):
        return slice(halo + t * rows, halo + (t + 1) * rows)

    def own_terms(r, day):
        matrix = r % 2
        pack(r, REACH, tiles_here)
        for t in range(tiles_here):
            v = wide[r, :, shifted(t)]
            both = dot_nt(packed[REACH + t], tiles_vm[matrix, t, 0])
            total = v + both[:tracers] + both[tracers:]
            if matrix == 1:
                at = (t * days + day) * tracers
                total += force[at : at + tracers, :rows] + force[at : at + tracers, rows:]
                for j in range(tracers):
                    total += jac_vm[day, j, :, at_tile(t)] * v[j : j + 1]
            base[:, at_tile(t)] = total

    def far_terms(r, chosen):
        matrix = r % 2
        for t in chosen:
            at = (matrix * tiles_here + t) * near
            picks = [packed[cols_ref[at + k]] for k in range(1, near)]
            stored = [tiles_vm[matrix, t, k] for k in range(1, near)]
            both = dot_nt(jnp.concatenate(picks, axis=1), jnp.concatenate(stored, axis=1))
            total = base[:, at_tile(t)] + both[:tracers] + both[tracers:]
            if r == rounds - 1:
                out_ref[0, :, at_tile(t)] = total
            else:
                wide[r + 1, :, shifted(t)] = total

    for r in range(rounds):
        day = days - 1 - r // 2
        if r == 0:
            body.wait_recv()
            loads[0].wait()
        if r == 1:
            loads[1].wait()
            loads[2].wait()
            gather_forcing()
        own_terms(r, day)
        sends[r][1].wait_recv()
        pack(r, 0, REACH)
        far_terms(r, range(0, REACH))
        if r < rounds - 1:
            sends[r + 1][0].start()
        sends[r][0].wait_recv()
        pack(r, REACH + tiles_here, REACH)
        far_terms(r, range(tiles_here - REACH, tiles_here))
        if r < rounds - 1:
            sends[r + 1][1].start()

    for pair in sends:
        for one in pair:
            one.wait_send()
    body.wait_send()

    @pl.loop(1, peers)
    def _(o):
        obs_copy(o).wait_send()


def on_device(
    seasons,
    peers,
    start_adjoint,
    adjoint_tiles,
    column_tiles,
    source_jacobian,
    obs_owner,
    obs_local,
    obs_day,
    obs_tracer,
    obs_misfit,
):
    days, tracers = source_jacobian.shape[1], source_jacobian.shape[2]
    tiles_here, near, rows = adjoint_tiles.shape[2], adjoint_tiles.shape[3], adjoint_tiles.shape[-1]
    cells_here = start_adjoint.shape[2]
    assert tiles_here == 2 * REACH
    wide_cells = cells_here + 2 * REACH * rows
    listed = obs_local.shape[1]
    rounds = 2 * days
    first_tile = lax.axis_index("cells") * tiles_here
    local_tiles = (column_tiles - first_tile + REACH) % (tiles_here * peers)
    vmem = pl.BlockSpec(memory_space=pltpu.VMEM)
    hbm = pl.BlockSpec(memory_space=pl.ANY)
    return pl.pallas_call(
        functools.partial(kernel, seasons, peers),
        out_shape=jax.ShapeDtypeStruct(start_adjoint.shape, F32),
        in_specs=[pl.BlockSpec(memory_space=pltpu.SMEM), hbm, hbm, hbm] + [vmem] * 5,
        out_specs=vmem,
        scratch_shapes=[
            pltpu.VMEM((2, tiles_here, near, rows, rows), BF16),
            pltpu.VMEM((days, tracers, tracers, cells_here), F32),
            pltpu.VMEM((rounds, tracers, wide_cells), F32),
            pltpu.VMEM((tiles_here + 2 * REACH, 2 * tracers, rows), BF16),
            pltpu.VMEM((tracers, cells_here), F32),
            pltpu.VMEM((peers, 4 * listed // rows, rows), F32),
            pltpu.VMEM((tiles_here * days * tracers, 2 * rows), F32),
            pltpu.SemaphoreType.DMA((3,)),
            pltpu.SemaphoreType.DMA((rounds, 3)),
            pltpu.SemaphoreType.DMA((rounds, 3)),
            pltpu.SemaphoreType.DMA((peers,)),
            pltpu.SemaphoreType.DMA((peers,)),
        ],
        compiler_params=pltpu.CompilerParams(collective_id=0, has_side_effects=True),
    )(
        local_tiles.reshape(-1),
        start_adjoint,
        adjoint_tiles,
        source_jacobian,
        obs_owner.reshape(1, listed),
        obs_local,
        obs_day,
        obs_tracer,
        obs_misfit,
    )


def solution(mesh):
    placed = (
        P("season", None, "cells"),
        P("season", None, "cells", None, None, None),
        P("season", None, "cells", None),
        P("season", None, None, None, "cells"),
        P("season", "cells", None),
        P("season", "cells"),
        P("season", "cells"),
        P("season", "cells"),
        P("season", "cells"),
    )
    return jax.shard_map(
        functools.partial(on_device, mesh.shape["season"], mesh.shape["cells"]),
        mesh=mesh,
        in_specs=placed,
        out_specs=P("season", None, "cells"),
        check_vma=False,
    )
```

time: 121 us -> 32.3 us (0.27)
  blocking collectives: 42.3 us -> 0 us
  other arithmetic: 35.2 us -> 0.7 us
  Pallas kernels: 0 us -> 29.2 us
  waiting for transfers between devices: 16.6 us -> 0 us
  matrix products: 10.7 us -> 0 us
  starting transfers between devices: 8.78 us -> 0 us
  local copies, waits for them, and re-layouts: 7.01 us -> 2.18 us
    all_gather x1 -> x0, blocking collectives: 42.3 us -> none  [on_device(): everything = lax.all_gather(packed, 'cells', axis=1, tiled=True)]
    pallas_call x0 -> x1, Pallas kernels: none -> 29.2 us  [on_device(): pl.pallas_call(functools.partial(kernel, seasons, peers), out_shape=jax.S...]
    scatter-add x1 -> x0, other arithmetic: 27.9 us -> none  [on_device(): jax.ops.segment_sum(arrived_values, arrived_keys, num_segments=forcing_sl...]
    ppermute x9 -> x0, waiting for transfers between devices: 16.6 us -> none  [the longest x4 14.6 us: with_halo(): lax.ppermute(tail, axis, [(i, (i + 1) % count) for i in range(count)])]
    dot_general x4 -> x0, matrix products: 10.7 us -> none  [apply_matrix(): jnp.einsum('tkac,rtkc->rta', matrix_tiles, picked, preferred_element_type...]
    ppermute x9 -> x0, starting transfers between devices: 8.78 us -> none  [the longest x4 8.05 us: with_halo(): lax.ppermute(tail, axis, [(i, (i + 1) % count) for i in range(count)])]
    slice x8 -> x0, local copies, waits for them, and re-layouts: 3.55 us -> none  [the longest x3 2.76 us: on_device(): forcing[day_index]]
    dot_general x2 -> x0, other arithmetic: 3.44 us -> none  [on_device(): jnp.einsum('jrc,jc->rc', source_jacobian[0, day_index], carried, precisio...]
  transfers between devices with their start and end apart: 9 -> 0, of which waited for: 8 -> 0; matrix products, arithmetic and copies ran while one was open for 31% -> 0% of each run, Pallas kernels for 0% -> 0%
where the time goes in v1:
time: 32.3 us; the launch traced here: 32.1 us
  Pallas kernels  29.2 us (90%)
  local copies, waits for them, and re-layouts  2.18 us (7%)
  other arithmetic  0.7 us (2%)
    pallas_call x1, Pallas kernels, on_device(): pl.pallas_call(functools.partial(kernel, seasons, peers), out_shape=jax.S...  29.2 us
    unnamed x1, local copies, waits for them, and re-layouts  1.47 us
    select_n x1, other arithmetic, on_device(): local_tiles = (column_tiles - first_tile + REACH) % (tiles_here * peers)  0.7 us

profile of v1, /device:TPU:0, one launch (start us, length us, event | category | flops | bytes accessed | tf_op | source)
XLA Modules:
  0.0 32.1 jit_solution(11538168617625476250)
XLA Ops:
  0.0 0.7 %and_select_fusion = s32[1,2,16,3]{2,1,3,0:T(2,128)S(1)} fusion(s32[1,2,16,3]{2,1,3,0:T(2,128)} %param.11, s32[]{:T(128)S(6)} %mul.3), kind=kLoop, calls=%fused_computation.2 | loop fusion | flops 1248 | bytes 772 | tf_op jit(solution)/shard_map/jit(remainder)/select_n | solution.py:259
  0.7 0.1 copy.11
  0.8 0.6 %reshape.6.cols_ref = s32[96]{0:T(128)} reshape(s32[1,2,16,3]{3,2,1,0:T(8,128)S(1)} %copy.11) | data formatting | bytes 768 | tf_op jit(solution)/shard_map/reshape | solution.py:283
  1.4 29.2 %shard_map.91 = f32[1,8,2048]{2,1,0:T(8,128)} custom-call(s32[96]{0:T(128)} %reshape.6.cols_ref, f32[1,8,2048]{2,1,0:T(8,128)} %start_ref.1, bf16[1,2,16,3,128,128]{5,4,3,2,1,0:T(8,128)(2,1)} %tiles_hbm.1, f32[1,2,8,8,2048]{4,3,2,1,0:T(8,128)} %jac_hbm.1, s32[1,256]{1,0:T(1,128)} %bitcast.3, s32[1,256]{1,0:T(1,128)} %local_ref.1, s32[1,256]{1,0:T(1,128)} %day_ref.1, ...), custom_call_target="tpu_custom_call" | custom-call | tf_op jit(solution)/shard_map/pallas_call | solution.py:262
  30.7 1.5 %copy.13 = f32[1,8,2048]{2,1,0:T(8,128)} copy(f32[1,8,2048]{2,1,0:T(8,128)} %shard_map.91) | data formatting | bytes 131072

commit v2 on v1

--- a/solution.py
+++ b/solution.py
@@ -8,6 +8,7 @@
 from jax.sharding import PartitionSpec as P
 
 REACH = 8
+PIECES = 2
 MESH = pl.DeviceIdType.MESH
 F32 = jnp.float32
 BF16 = jnp.bfloat16
@@ -20,10 +21,17 @@
 def kernel(
     seasons,
     peers,
-    cols_ref,
+    cols_hbm,
     start_ref,
     tiles_hbm,
     jac_hbm,
+    owner_hbm,
+    local_hbm,
+    day_hbm,
+    tracer_hbm,
+    misfit_hbm,
+    out_hbm,
+    cols_ref,
     owner_ref,
     local_ref,
     day_ref,
@@ -38,6 +46,7 @@
     obs,
     force,
     load_sem,
+    store_sem,
     send_sem,
     recv_sem,
     obs_send_sem,
@@ -50,16 +59,11 @@
     rows = tiles_vm.shape[-1]
     cells_here = tiles_here * rows
     halo = REACH * rows
+    total_tiles = tiles_here * peers
+    piece = halo // PIECES
+    step = REACH // PIECES
     rounds = 2 * days
     own = slice(halo, halo + cells_here)
-
-    loads = [
-        pltpu.make_async_copy(tiles_hbm.at[0, 0], tiles_vm.at[0], load_sem.at[0]),
-        pltpu.make_async_copy(tiles_hbm.at[0, 1], tiles_vm.at[1], load_sem.at[1]),
-        pltpu.make_async_copy(jac_hbm.at[0], jac_vm, load_sem.at[2]),
-    ]
-    for load in loads:
-        load.start()
 
     met = {(0, o) for o in range(1, peers)}
     met |= {(ds % seasons, dc % peers) for ds in (1, -1) for dc in (-1, 0, 1)}
@@ -73,6 +77,23 @@
             device_id_type=MESH,
         )
 
+    pairs = (
+        (owner_hbm, owner_ref),
+        (local_hbm, local_ref),
+        (day_hbm, day_ref),
+        (tracer_hbm, tracer_ref),
+        (misfit_hbm, misfit_ref),
+        (cols_hbm, cols_ref),
+        (tiles_hbm.at[0, 0], tiles_vm.at[0]),
+        (tiles_hbm.at[0, 1], tiles_vm.at[1]),
+        (jac_hbm.at[0], jac_vm),
+    )
+    loads = [pltpu.make_async_copy(a, b, load_sem.at[i]) for i, (a, b) in enumerate(pairs)]
+    for load in loads:
+        load.start()
+    for load in loads[:5]:
+        load.wait()
+
     shift = rows.bit_length() - 1
     local = local_ref[...]
     row_key = (local >> shift) * (days * tracers) + day_ref[...] * tracers + tracer_ref[...]
@@ -101,16 +122,21 @@
 
     def halo_copies(r):
         season = before if r == 0 else s
-        if r == 0:
-            head = start_ref.at[0, :, 0:halo]
-            tail = start_ref.at[0, :, cells_here - halo : cells_here]
-        else:
-            head = wide.at[r, :, halo : 2 * halo]
-            tail = wide.at[r, :, cells_here : halo + cells_here]
-        return (
-            copy(head, r, slice(halo + cells_here, 2 * halo + cells_here), season, left, 0),
-            copy(tail, r, slice(0, halo), season, right, 1),
-        )
+        copies = []
+        for i in range(PIECES):
+            at = i * piece
+            if r == 0:
+                head = start_ref.at[0, :, at : at + piece]
+                tail = start_ref.at[0, :, cells_here - halo + at : cells_here - halo + at + piece]
+            else:
+                head = wide.at[r, :, halo + at : halo + at + piece]
+                tail = wide.at[r, :, cells_here + at : cells_here + at + piece]
+            behind = halo + cells_here + at
+            copies += [
+                copy(head, r, slice(behind, behind + piece), season, left, 2 * i),
+                copy(tail, r, slice(at, at + piece), season, right, 2 * i + 1),
+            ]
+        return copies
 
     def obs_copy(o):
         return pltpu.make_async_remote_copy(
@@ -123,11 +149,11 @@
         )
 
     sends = [halo_copies(r) for r in range(rounds)]
-    body = copy(start_ref.at[0], 0, own, before, c, 2)
+    body = copy(start_ref.at[0], 0, own, before, c, 2 * PIECES)
 
     pl.semaphore_wait(barrier, len(met))
-    sends[0][0].start()
-    sends[0][1].start()
+    for one in sends[0]:
+        one.start()
     body.start()
 
     @pl.loop(1, peers)
@@ -194,40 +220,61 @@
     def far_terms(r, chosen):
         matrix = r % 2
         for t in chosen:
-            at = (matrix * tiles_here + t) * near
-            picks = [packed[cols_ref[at + k]] for k in range(1, near)]
+            picks = []
+            for k in range(1, near):
+                ahead = cols_ref[0, k, matrix, t] + (total_tiles + REACH - c * tiles_here)
+                if total_tiles & (total_tiles - 1) == 0:
+                    ahead = ahead & (total_tiles - 1)
+                else:
+                    ahead = lax.rem(ahead, total_tiles)
+                picks.append(packed[jnp.minimum(ahead, packed.shape[0] - 1)])
             stored = [tiles_vm[matrix, t, k] for k in range(1, near)]
             both = dot_nt(jnp.concatenate(picks, axis=1), jnp.concatenate(stored, axis=1))
             total = base[:, at_tile(t)] + both[:tracers] + both[tracers:]
             if r == rounds - 1:
-                out_ref[0, :, at_tile(t)] = total
+                out_ref[:, at_tile(t)] = total
             else:
                 wide[r + 1, :, shifted(t)] = total
+
+    stores = [
+        pltpu.make_async_copy(
+            out_ref.at[:, i * halo : (i + 1) * halo],
+            out_hbm.at[0, :, i * halo : (i + 1) * halo],
+            store_sem.at[i],
+        )
+        for i in range(2)
+    ]
 
     for r in range(rounds):
         day = days - 1 - r // 2
         if r == 0:
             body.wait_recv()
-            loads[0].wait()
+            loads[6].wait()
         if r == 1:
-            loads[1].wait()
-            loads[2].wait()
+            loads[7].wait()
+            loads[8].wait()
             gather_forcing()
         own_terms(r, day)
-        sends[r][1].wait_recv()
-        pack(r, 0, REACH)
-        far_terms(r, range(0, REACH))
-        if r < rounds - 1:
-            sends[r + 1][0].start()
-        sends[r][0].wait_recv()
-        pack(r, REACH + tiles_here, REACH)
-        far_terms(r, range(tiles_here - REACH, tiles_here))
-        if r < rounds - 1:
-            sends[r + 1][1].start()
-
-    for pair in sends:
-        for one in pair:
+        if r == 0:
+            loads[5].wait()
+        for side in (0, 1):
+            lands = REACH + tiles_here if side else 0
+            from_tile = tiles_here - REACH if side else 0
+            for i in range(PIECES):
+                sends[r][2 * i + 1 - side].wait_recv()
+                pack(r, lands + i * step, step)
+            for i in range(PIECES):
+                far_terms(r, range(from_tile + i * step, from_tile + (i + 1) * step))
+                if r < rounds - 1:
+                    sends[r + 1][2 * i + side].start()
+            if r == rounds - 1:
+                stores[side].start()
+
+    for group in sends:
+        for one in group:
             one.wait_send()
+    for store in stores:
+        store.wait()
     body.wait_send()
 
     @pl.loop(1, peers)
@@ -255,16 +302,19 @@
     wide_cells = cells_here + 2 * REACH * rows
     listed = obs_local.shape[1]
     rounds = 2 * days
-    first_tile = lax.axis_index("cells") * tiles_here
-    local_tiles = (column_tiles - first_tile + REACH) % (tiles_here * peers)
-    vmem = pl.BlockSpec(memory_space=pltpu.VMEM)
     hbm = pl.BlockSpec(memory_space=pl.ANY)
     return pl.pallas_call(
         functools.partial(kernel, seasons, peers),
         out_shape=jax.ShapeDtypeStruct(start_adjoint.shape, F32),
-        in_specs=[pl.BlockSpec(memory_space=pltpu.SMEM), hbm, hbm, hbm] + [vmem] * 5,
-        out_specs=vmem,
+        in_specs=[hbm] * 9,
+        out_specs=hbm,
         scratch_shapes=[
+            pltpu.SMEM((1, near, 2, tiles_here), jnp.int32),
+        ]
+        + [pltpu.VMEM((1, listed), jnp.int32)] * 4
+        + [
+            pltpu.VMEM((1, listed), F32),
+            pltpu.VMEM((tracers, cells_here), F32),
             pltpu.VMEM((2, tiles_here, near, rows, rows), BF16),
             pltpu.VMEM((days, tracers, tracers, cells_here), F32),
             pltpu.VMEM((rounds, tracers, wide_cells), F32),
@@ -272,15 +322,16 @@
             pltpu.VMEM((tracers, cells_here), F32),
             pltpu.VMEM((peers, 4 * listed // rows, rows), F32),
             pltpu.VMEM((tiles_here * days * tracers, 2 * rows), F32),
-            pltpu.SemaphoreType.DMA((3,)),
-            pltpu.SemaphoreType.DMA((rounds, 3)),
-            pltpu.SemaphoreType.DMA((rounds, 3)),
+            pltpu.SemaphoreType.DMA((9,)),
+            pltpu.SemaphoreType.DMA((2,)),
+            pltpu.SemaphoreType.DMA((rounds, 2 * PIECES + 1)),
+            pltpu.SemaphoreType.DMA((rounds, 2 * PIECES + 1)),
             pltpu.SemaphoreType.DMA((peers,)),
             pltpu.SemaphoreType.DMA((peers,)),
         ],
         compiler_params=pltpu.CompilerParams(collective_id=0, has_side_effects=True),
     )(
-        local_tiles.reshape(-1),
+        column_tiles.transpose(0, 3, 1, 2),
         start_adjoint,
         adjoint_tiles,
         source_jacobian,

time: 32.3 us -> 30 us (0.929)
  Pallas kernels: 29.2 us -> 28.3 us
  local copies, waits for them, and re-layouts: 2.18 us -> 1.47 us
  other arithmetic: 0.7 us -> 0 us
    pallas_call x1, Pallas kernels: 29.2 us -> 28.3 us  [on_device(): pl.pallas_call(functools.partial(kernel, seasons, peers), out_shape=jax.S...]
    select_n x1 -> x0, other arithmetic: 0.7 us -> none  [on_device(): local_tiles = (column_tiles - first_tile + REACH) % (tiles_here * peers)]
    reshape x1 -> x0, local copies, waits for them, and re-layouts: 0.62 us -> none  [on_device(): local_tiles.reshape(-1)]
where the time goes in v2:
time: 30 us; the launch traced here: 29.8 us
  Pallas kernels  28.3 us (94%)
  local copies, waits for them, and re-layouts  1.47 us (5%)
    pallas_call x1, Pallas kernels, on_device(): pl.pallas_call(functools.partial(kernel, seasons, peers), out_shape=jax.S...  28.3 us
    unnamed x1, local copies, waits for them, and re-layouts  1.47 us

profile of v2, /device:TPU:0, one launch (start us, length us, event | category | flops | bytes accessed | tf_op | source)
XLA Modules:
  0.0 29.8 jit_solution(2347563277686877736)
XLA Ops:
  0.0 28.3 %shard_map.91 = f32[1,8,2048]{2,1,0:T(8,128)} custom-call(s32[1,3,2,16]{3,2,1,0:T(2,128)} %bitcast.2, f32[1,8,2048]{2,1,0:T(8,128)} %start_ref.1, bf16[1,2,16,3,128,128]{5,4,3,2,1,0:T(8,128)(2,1)} %tiles_hbm.1, f32[1,2,8,8,2048]{4,3,2,1,0:T(8,128)} %jac_hbm.1, s32[1,256]{1,0:T(1,128)} %bitcast.3, s32[1,256]{1,0:T(1,128)} %local_hbm.1, s32[1,256]{1,0:T(1,128)} %day_hbm.1, ...), custom_call_target="tpu_custom_call" | custom-call | tf_op jit(solution)/shard_map/pallas_call | solution.py:306
  28.3 1.5 %copy.11 = f32[1,8,2048]{2,1,0:T(8,128)} copy(f32[1,8,2048]{2,1,0:T(8,128)} %shard_map.91) | data formatting | bytes 131072

commit v3 on v2

--- a/solution.py
+++ b/solution.py
@@ -156,10 +156,6 @@
         one.start()
     body.start()
 
-    @pl.loop(1, peers)
-    def _(o):
-        obs_copy(o).start()
-
     def pack(r, first, count):
         for t in range(first, first + count):
             v = wide[r, :, at_tile(t)]
@@ -232,18 +228,9 @@
             both = dot_nt(jnp.concatenate(picks, axis=1), jnp.concatenate(stored, axis=1))
             total = base[:, at_tile(t)] + both[:tracers] + both[tracers:]
             if r == rounds - 1:
-                out_ref[:, at_tile(t)] = total
+                out_hbm[0, :, at_tile(t)] = total
             else:
                 wide[r + 1, :, shifted(t)] = total
-
-    stores = [
-        pltpu.make_async_copy(
-            out_ref.at[:, i * halo : (i + 1) * halo],
-            out_hbm.at[0, :, i * halo : (i + 1) * halo],
-            store_sem.at[i],
-        )
-        for i in range(2)
-    ]
 
     for r in range(rounds):
         day = days - 1 - r // 2
@@ -257,6 +244,11 @@
         own_terms(r, day)
         if r == 0:
             loads[5].wait()
+
+            @pl.loop(1, peers)
+            def _(o):
+                obs_copy(o).start()
+
         for side in (0, 1):
             lands = REACH + tiles_here if side else 0
             from_tile = tiles_here - REACH if side else 0
@@ -267,14 +259,10 @@
                 far_terms(r, range(from_tile + i * step, from_tile + (i + 1) * step))
                 if r < rounds - 1:
                     sends[r + 1][2 * i + side].start()
-            if r == rounds - 1:
-                stores[side].start()
 
     for group in sends:
         for one in group:
             one.wait_send()
-    for store in stores:
-        store.wait()
     body.wait_send()
 
     @pl.loop(1, peers)
@@ -305,9 +293,9 @@
     hbm = pl.BlockSpec(memory_space=pl.ANY)
     return pl.pallas_call(
         functools.partial(kernel, seasons, peers),
-        out_shape=jax.ShapeDtypeStruct(start_adjoint.shape, F32),
+        out_shape=pltpu.VMEM(start_adjoint.shape, F32),
         in_specs=[hbm] * 9,
-        out_specs=hbm,
+        out_specs=pl.BlockSpec(memory_space=pltpu.VMEM),
         scratch_shapes=[
             pltpu.SMEM((1, near, 2, tiles_here), jnp.int32),
         ]

time: 30 us -> 28.3 us (0.943)
  local copies, waits for them, and re-layouts: 1.47 us -> 0.63 us
  Pallas kernels: 28.3 us -> 27.5 us
    unnamed x1, local copies, waits for them, and re-layouts: 1.47 us -> 0.63 us
    pallas_call x1, Pallas kernels: 28.3 us -> 27.5 us  [on_device(): pl.pallas_call(functools.partial(kernel, seasons, peers), out_shape=pltpu...]
where the time goes in v3:
time: 28.3 us; the launch traced here: 28.1 us
  Pallas kernels  27.5 us (97%)
  local copies, waits for them, and re-layouts  0.63 us (2%)
    pallas_call x1, Pallas kernels, on_device(): pl.pallas_call(functools.partial(kernel, seasons, peers), out_shape=pltpu...  27.5 us
    unnamed x1, local copies, waits for them, and re-layouts  0.63 us

profile of v3, /device:TPU:0, one launch (start us, length us, event | category | flops | bytes accessed | tf_op | source)
XLA Modules:
  0.0 28.1 jit_solution(14260641254988839772)
XLA Ops:
  0.0 27.5 %shard_map.91 = f32[1,8,2048]{2,1,0:T(8,128)S(1)} custom-call(s32[1,3,2,16]{3,2,1,0:T(2,128)} %bitcast.2, f32[1,8,2048]{2,1,0:T(8,128)} %start_ref.1, bf16[1,2,16,3,128,128]{5,4,3,2,1,0:T(8,128)(2,1)} %tiles_hbm.1, f32[1,2,8,8,2048]{4,3,2,1,0:T(8,128)} %jac_hbm.1, s32[1,256]{1,0:T(1,128)} %bitcast.3, s32[1,256]{1,0:T(1,128)} %local_hbm.1, s32[1,256]{1,0:T(1,128)} %day_hbm.1, ...), custom_call_target="tpu_custom_call" | custom-call | tf_op jit(solution)/shard_map/pallas_call | solution.py:294
  27.5 0.6 %copy.11 = f32[1,8,2048]{2,1,0:T(8,128)} copy(f32[1,8,2048]{2,1,0:T(8,128)S(1)} %shard_map.91) | data formatting | bytes 131072
